TPU v7x, 32 devices: a whole 2x2x4 slice. The times are simulated.
32 devices in a mesh: seq: 4 (over y, x), head: 4 (over z), rep: 2 (over core).
Axes of the slice: x: 2, y: 2, z: 4, core: 2. Of those that a mesh axis runs over, the one named last changes fastest.
Arguments:
- query_heads: bfloat16 [2, 8192, 4096], P('rep', 'seq', 'head'), may hold values from -0.59765625 to 0.59765625
- key_heads: bfloat16 [2, 8192, 4096], P('rep', 'seq', 'head'), may hold values from -0.59765625 to 0.59765625
- value_heads: bfloat16 [2, 8192, 4096], P('rep', 'seq', 'head'), may hold values from -6 to 6
- out_cotangent: bfloat16 [2, 8192, 4096], P('rep', 'seq', 'head'), may hold values from -0.19921875 to 0.19921875
- out_weight: bfloat16 [4096, 4096], P('head'), may hold values from -0.09375 to 0.09375
- doc_ends: int32 [2, 7], P('rep'), may hold values from 1 to 8192, as said below
Outputs:
- grad_query: bfloat16 [2, 8192, 4096], P('rep', 'seq', 'head')
- grad_key: bfloat16 [2, 8192, 4096], P('rep', 'seq', 'head')
- grad_value: bfloat16 [2, 8192, 4096], P('rep', 'seq', 'head')
- grad_weight: float32 [4096, 4096], P('head', ('seq', 'rep'))
Inputs may be any that keep to these rules, and one draw needn't show every extreme that they name: `doc_ends`: each row holds 7 strictly increasing document end offsets; its last entry is 8192.
All inputs are finite; a program needn't handle non-finite values.
Results may differ from a plain program's by a relative error of at most 0.0052.
Values may be sent and summed in bfloat16 or wider, within the bound.
No kernel may reach another device: no remote copies, remote signals or barrier semaphores. Data moves between devices by JAX's collectives and lax.ppermute only.
A program may use at most 320 MiB of HBM per device.

v0:
```python
import jax
import jax.numpy as jnp
from jax import lax
from jax.sharding import PartitionSpec as P

HD = 128
BLOCK = 512
highest = lax.Precision.HIGHEST


def prefix(shard, axis, combine, identity, reverse):
    count, here = (lax.axis_size(axis), lax.axis_index(axis))
    everything = jax.tree.map(lambda part: lax.all_gather(part, axis), shard)
    start = jax.tree.map(
        lambda part, zero: jnp.broadcast_to(jnp.asarray(zero, part.dtype), part.shape),
        shard,
        identity,
    )

    def step(k, before):
        at = count - 1 - k if reverse else k
        reached = at > here if reverse else at < here
        new = combine(before, jax.tree.map(lambda part: part[at], everything))
        return jax.tree.map(lambda a, b: jnp.where(reached, a, b), new, before)

    return lax.fori_loop(0, count, step, start)


def doc_counts(positions, ends_row):
    return jnp.sum((ends_row[None, :] <= positions[:, None]).astype(jnp.int32), axis=1)


def local_pass(queries, keys, values, grads, counts, count_before):
    length, heads, width = queries.shape
    blocks = length // BLOCK
    query_blocks = queries.reshape(blocks, BLOCK, heads, width)
    key_blocks = keys.reshape(blocks, BLOCK, heads, width)
    value_blocks = values.reshape(blocks, BLOCK, heads, width)
    grad_blocks = grads.reshape(blocks, BLOCK, heads, width)
    count_blocks = counts.reshape(blocks, BLOCK)
    before_each = jnp.concatenate([jnp.reshape(count_before, (1,)), count_blocks[:-1, -1]])
    last_each = count_blocks[:, -1]
    rows = lax.broadcasted_iota(jnp.int32, (BLOCK, BLOCK), 0)
    cols = lax.broadcasted_iota(jnp.int32, (BLOCK, BLOCK), 1)
    allowed = (
        (count_blocks[:, :, None] == count_blocks[:, None, :]) & (rows >= cols)[None]
    ).astype(jnp.float32)
    scores = jnp.einsum(
        "nthe,nshe->nhts", query_blocks, key_blocks, preferred_element_type=jnp.float32
    )
    attn = (scores * allowed[:, None]).astype(jnp.bfloat16)
    back = jnp.einsum(
        "nthe,nshe->nhts", grad_blocks, value_blocks, preferred_element_type=jnp.float32
    )
    pgrad = (back * allowed[:, None]).astype(jnp.bfloat16)
    out_intra = jnp.einsum(
        "nhts,nshe->nthe", attn, value_blocks, preferred_element_type=jnp.float32
    )
    dq_intra = jnp.einsum("nhts,nshe->nthe", pgrad, key_blocks, preferred_element_type=jnp.float32)
    dk_intra = jnp.einsum(
        "nhts,nthe->nshe", pgrad, query_blocks, preferred_element_type=jnp.float32
    )
    dv_intra = jnp.einsum("nhts,nthe->nshe", attn, grad_blocks, preferred_element_type=jnp.float32)
    first_match = (count_blocks == before_each[:, None])[:, :, None, None]
    last_match = (count_blocks == last_each[:, None])[:, :, None, None]
    keep = (last_each == before_each).astype(jnp.float32)
    tails = jnp.einsum(
        "nshe,nshf->nhef",
        key_blocks * last_match.astype(jnp.bfloat16),
        value_blocks,
        preferred_element_type=jnp.float32,
    )
    head_sums = jnp.einsum(
        "nthe,nthf->nhef",
        query_blocks * first_match.astype(jnp.bfloat16),
        grad_blocks,
        preferred_element_type=jnp.float32,
    )

    def link_step(state, item):
        return (item[0] + item[1] * state, state)

    empty = jnp.zeros((heads, width, width), jnp.float32)
    final_tail, states_before = lax.scan(link_step, empty, (tails, keep))
    final_head, states_after = lax.scan(link_step, empty, (head_sums, keep), reverse=True)
    first_weight = first_match.astype(jnp.float32)
    last_weight = last_match.astype(jnp.float32)
    outputs = out_intra + first_weight * jnp.einsum(
        "nthe,nhef->nthf", query_blocks.astype(jnp.float32), states_before, precision=highest
    )
    dq = dq_intra + first_weight * jnp.einsum(
        "nthf,nhef->nthe", grad_blocks.astype(jnp.float32), states_before, precision=highest
    )
    dk = dk_intra + last_weight * jnp.einsum(
        "nshf,nhef->nshe", value_blocks.astype(jnp.float32), states_after, precision=highest
    )
    dv = dv_intra + last_weight * jnp.einsum(
        "nshe,nhef->nshf", key_blocks.astype(jnp.float32), states_after, precision=highest
    )
    shape = (length, heads, width)
    return (
        outputs.reshape(shape),
        dq.reshape(shape),
        dk.reshape(shape),
        dv.reshape(shape),
        final_tail,
        final_head,
    )


def link_states(earlier, later):
    return (jnp.maximum(earlier[0], later[0]), later[1] + (1.0 - later[0]) * earlier[1])


def on_device(query_heads, key_heads, value_heads, out_cotangent, out_weight, doc_ends):
    length = query_heads.shape[1]
    heads = query_heads.shape[2] // HD
    queries = query_heads[0].reshape(length, heads, HD)
    keys = key_heads[0].reshape(length, heads, HD)
    values = value_heads[0].reshape(length, heads, HD)
    full_cotangent = lax.all_gather(out_cotangent, "head", axis=2, tiled=True)[0]
    grads_flat = lax.dot_general(
        full_cotangent, out_weight, (((1,), (1,)), ((), ())), preferred_element_type=jnp.float32
    ).astype(jnp.bfloat16)
    grads = grads_flat.reshape(length, heads, HD)
    offset = lax.axis_index("seq") * length
    positions = offset + jnp.arange(length, dtype=jnp.int32)
    ends_row = doc_ends[0]
    counts = doc_counts(positions, ends_row)
    count_before = doc_counts(jnp.reshape(offset - 1, (1,)), ends_row)[0]
    outputs, dq, dk, dv, tail, head = local_pass(queries, keys, values, grads, counts, count_before)
    flag = (counts[-1] != count_before).astype(jnp.float32)
    identity = (jnp.zeros((), jnp.float32), jnp.zeros_like(tail))
    flag_before, carry_before = prefix((flag, tail), "seq", link_states, identity, False)
    flag_after, carry_after = prefix((flag, head), "seq", link_states, identity, True)
    entry_weight = (counts == count_before).astype(jnp.float32)[:, None, None]
    exit_weight = (counts == counts[-1]).astype(jnp.float32)[:, None, None]
    outputs = outputs + entry_weight * jnp.einsum(
        "the,hef->thf", queries.astype(jnp.float32), carry_before, precision=highest
    )
    dq = dq + entry_weight * jnp.einsum(
        "thf,hef->the", grads.astype(jnp.float32), carry_before, precision=highest
    )
    dk = dk + exit_weight * jnp.einsum(
        "thf,hef->the", values.astype(jnp.float32), carry_after, precision=highest
    )
    dv = dv + exit_weight * jnp.einsum(
        "the,hef->thf", keys.astype(jnp.float32), carry_after, precision=highest
    )
    flat = heads * HD
    attention_out = outputs.reshape(length, flat).astype(jnp.bfloat16)
    grad_query = dq.reshape(1, length, flat).astype(jnp.bfloat16)
    grad_key = dk.reshape(1, length, flat).astype(jnp.bfloat16)
    grad_value = dv.reshape(1, length, flat).astype(jnp.bfloat16)
    partial_grad = lax.dot_general(
        attention_out, full_cotangent, (((0,), (0,)), ((), ())), preferred_element_type=jnp.float32
    )
    summed = lax.psum(partial_grad, ("seq", "rep"))
    columns = summed.shape[1] // lax.axis_size(("seq", "rep"))
    grad_weight = lax.dynamic_slice_in_dim(
        summed, lax.axis_index(("seq", "rep")) * columns, columns, 1
    )
    return (grad_query, grad_key, grad_value, grad_weight)


def solution(mesh):
    in_specs = (
        P("rep", "seq", "head"),
        P("rep", "seq", "head"),
        P("rep", "seq", "head"),
        P("rep", "seq", "head"),
        P("head", None),
        P("rep", None),
    )
    out_specs = (
        P("rep", "seq", "head"),
        P("rep", "seq", "head"),
        P("rep", "seq", "head"),
        P("head", ("seq", "rep")),
    )
    return jax.shard_map(
        on_device, mesh=mesh, in_specs=in_specs, out_specs=out_specs, check_vma=False
    )
```

profile of v0, /device:TPU:0, one launch (start us, length us, event | category | flops | bytes accessed | tf_op | source)
XLA Modules:
  0.0 711.5 jit_solution(5314023280602779764)
XLA Ops:
  33.0 10.0 %while.60 = (s32[]{:T(128)}, f32[8,128,128]{2,1,0:T(8,128)S(1)}, f32[4,8,128,128]{3,2,1,0:T(8,128)S(1)}, f32[4,8,128,128]{3,2,1,0:T(8,128)}, f32[4]{0:T(128)S(1)}, /*index=5*/s32[]{:T(128)}, s32[]{:T(128)}) while((s32[]{:T(128)}, f32[8,128,128]{2,1,0:T(8,128)S(1)}, f32[4,8,128,128]{3,2,1,0:T(8,128)S(1)}, ...), condition=%wide.region_3.4_spmd.clone, body=%wide.region_2.3_spmd.clone.sunk | while | flops 524291 | bytes 2621560 | solution.py:84
  48.1 11.7 %all-reduce = f32[4]{0:T(128)S(1)} all-reduce(f32[4]{0:T(128)S(1)} %dynamic-update-slice), channel_id=1, replica_groups=mesh['seq'=4,'head'=4,'rep'=2] {'seq'}, use_global_device_ids=true, to_apply=%add | all-reduce | flops 4 | bytes 32
  75.2 11.6 %multiply_convert_fusion = bf16[4,8,512,512]{3,2,1,0:T(8,128)(2,1)} fusion(f32[4,512,512]{2,1,0:T(8,128)} %and_convert_fusion, bf16[4,512,8,128]{1,3,2,0:T(8,128)(2,1)} %copy.184, bf16[4,512,8,128]{1,3,2,0:T(8,128)(2,1)} %copy.175), kind=kOutput, calls=%fused_computation.8 | convolution fusion | flops 2164260864 | bytes 29360128 | tf_op jit(solution)/shard_map/nthe,nshe->nhts/dot_general | solution.py:48
  86.8 17.2 %fusion.24 = f32[4,8,512,128]{3,2,1,0:T(8,128)} fusion(bf16[4,8,512,512]{3,2,1,0:T(8,128)(2,1)} %multiply_convert_fusion, bf16[4,512,8,128]{3,2,1,0:T(8,128)(2,1)} %bitcast.138), kind=kOutput, calls=%fused_computation.39 | convolution fusion | flops 2147483648 | bytes 29360128 | tf_op jit(solution)/shard_map/nhts,nshe->nthe/dot_general | solution.py:56
  131.8 11.0 %while.61 = (s32[]{:T(128)}, f32[8,128,128]{2,1,0:T(8,128)S(1)}, s32[]{:T(128)}, f32[4,8,128,128]{3,2,1,0:T(8,128)}, f32[4]{0:T(128)S(1)}, /*index=5*/s32[]{:T(128)}, f32[1]{0:T(128)}, s32[]{:T(128)}) while((s32[]{:T(128)}, f32[8,128,128]{2,1,0:T(8,128)S(1)}, s32[]{:T(128)}, f32[4,8,128,128]{3,2,1,0:T(8,128)}, f32[4]{0:T(128)S(1)}, ...), condition=%wide.region_5.6_spmd.clone, body=%wide.region_4.5_spmd.clone.sunk | while | flops 524293 | bytes 1573009 | solution.py:26
  142.8 10.8 %fusion.6 = bf16[2048,8,128]{0,2,1:T(8,128)(2,1)} fusion(f32[2048,8,128]{0,2,1:T(8,128)} %copy.209, f32[8,128,128]{2,1,0:T(8,128)S(1)} %get-tuple-element.364, bf16[2048,8,128]{2,1,0:T(8,128)(2,1)} %bitcast.145, f32[2048]{0:T(1024)S(1)} %get-tuple-element.507), kind=kOutput, calls=%fused_computation.15 | convolution fusion | flops 3227516928 | bytes 17309696 | tf_op jit(solution)/shard_map/the,hef->thf/dot_general | solution.py:138
  153.6 216.7 %all-gather.6.cloned.1.call-done = bf16[1,2048,4096]{2,1,0:T(8,128)(2,1)} async-done(((bf16[1,2048,1024]{2,1,0:T(8,128)(2,1)}), bf16[1,2048,4096]{2,1,0:T(8,128)(2,1)}) %all-gather.6.cloned.1.call-update) | async-done | bytes 16777232 | tf_op jit(solution)/shard_map/all_gather | solution.py:121
  370.3 24.1 %fusion.17 = bf16[2048,1024]{0,1:T(8,128)(2,1)} fusion(bf16[1024,4096]{1,0:T(8,128)(2,1)} %param.18, bf16[1,2048,4096]{2,1,0:T(8,128)(2,1)} %all-gather.6.cloned.1.call-done), kind=kOutput, calls=%fused_computation.34 | convolution fusion | flops 17181966336 | bytes 29360128 | tf_op jit(solution)/shard_map/dot_general | solution.py:122
  402.2 11.6 %multiply_convert_fusion.1 = bf16[4,8,512,512]{3,2,1,0:T(8,128)(2,1)} fusion(f32[4,512,512]{2,1,0:T(8,128)} %and_convert_fusion, bf16[4,512,8,128]{1,0,3,2:T(4,128)(2,1)} %reshape_reshape.3, bf16[4,512,8,128]{3,2,1,0:T(8,128)(2,1)} %bitcast.139), kind=kOutput, calls=%fused_computation.9 | convolution fusion | flops 2164260864 | bytes 29360128 | tf_op jit(solution)/shard_map/nthe,nshe->nhts/dot_general | solution.py:52
  413.9 14.7 %fusion.34 = f32[4,8,512,128]{3,2,1,0:T(8,128)} fusion(bf16[4,8,512,512]{3,2,1,0:T(8,128)(2,1)} %multiply_convert_fusion.1, bf16[4,512,8,128]{1,3,2,0:T(8,128)(2,1)} %copy.175), kind=kOutput, calls=%fused_computation.62 | convolution fusion | flops 2147483648 | bytes 29360128 | tf_op jit(solution)/shard_map/nhts,nshe->nthe/dot_general | solution.py:59
  435.3 10.6 %while.62 = (s32[]{:T(128)}, f32[8,128,128]{2,1,0:T(8,128)S(1)}, f32[4,8,128,128]{3,2,1,0:T(8,128)S(1)}, f32[4,8,128,128]{3,2,1,0:T(8,128)}, f32[4]{0:T(128)S(1)}, /*index=5*/s32[]{:T(128)}, s32[]{:T(128)}, s32[]{:T(128)}) while((s32[]{:T(128)}, f32[8,128,128]{2,1,0:T(8,128)S(1)}, f32[4,8,128,128]{3,2,1,0:T(8,128)S(1)}, ...), condition=%wide.region_7.8_spmd.clone, body=%wide.region_6.7_spmd.clone.sunk | while | flops 524292 | bytes 2621580 | solution.py:85
  446.8 23.6 %fusion.2 = f32[1024,4096]{1,0:T(8,128)} fusion(bf16[2048,1024]{0,1:T(8,128)(2,1)} %bitcast.157, bf16[1,2048,4096]{2,1,0:T(8,128)(2,1)} %all-gather.6.cloned.1.call-done), kind=kOutput, calls=%fused_computation.10 | convolution fusion | flops 17179869184 | bytes 37748736 | tf_op jit(solution)/shard_map/dot_general | solution.py:155
  470.4 9.9 %bitcast_add_fusion.10 = f32[4,512,8,128]{3,1,2,0:T(8,128)S(1)} fusion(f32[4,8,512,128]{3,2,1,0:T(8,128)} %fusion.34, f32[4,512]{1,0:T(4,128)S(1)} %convert_element_type.133, f32[4,8,128,128]{3,2,1,0:T(8,128)} %copy-done.3, bf16[4,512,8,128]{1,0,3,2:T(4,128)(2,1)} %reshape_reshape.3), kind=kOutput, calls=%fused_computation.24 | convolution fusion | flops 3225419776 | bytes 23076864 | tf_op jit(solution)/shard_map/nthf,nhef->nthe/dot_general | solution.py:91
  488.4 9.9 %copy.181 = f32[2048,8,128]{0,2,1:T(8,128)} copy(f32[2048,8,128]{2,1,0:T(8,128)} %bitcast.147) | data formatting | bytes 16777216 | tf_op jit(solution)/shard_map/reshape | solution.py:103
  498.2 10.8 %fusion.9 = bf16[2048,8,128]{0,2,1:T(8,128)(2,1)} fusion(f32[2048,8,128]{0,2,1:T(8,128)} %copy.181, f32[8,128,128]{2,1,0:T(8,128)S(1)} %get-tuple-element.364, bf16[2048,8,128]{0,2,1:T(8,128)(2,1)} %bitcast.150, f32[2048]{0:T(1024)S(1)} %get-tuple-element.507), kind=kOutput, calls=%fused_computation.23 | convolution fusion | flops 3227516928 | bytes 17309696 | tf_op jit(solution)/shard_map/thf,hef->the/dot_general | solution.py:141
  515.5 11.9 %fusion.35 = f32[4,8,512,128]{3,2,1,0:T(8,128)} fusion(bf16[4,8,512,512]{3,2,1,0:T(8,128)(2,1)} %multiply_convert_fusion.1, bf16[4,512,8,128]{1,3,2,0:T(8,128)(2,1)} %copy.184), kind=kOutput, calls=%fused_computation.63 | convolution fusion | flops 2147483648 | bytes 29360128 | tf_op jit(solution)/shard_map/nhts,nthe->nshe/dot_general | solution.py:60
  543.6 9.4 %copy.190 = f32[2048,8,128]{0,2,1:T(8,128)} copy(f32[2048,8,128]{2,1,0:T(8,128)} %bitcast.148) | data formatting | bytes 16777216 | tf_op jit(solution)/shard_map/reshape | solution.py:104
  560.7 17.0 %add_bitcast_fusion = f32[4,512,8,128]{3,1,2,0:T(8,128)} fusion(f32[4,8,128,512]{2,3,1,0:T(8,128)} %fusion.36, f32[4,512]{1,0:T(4,128)S(1)} %copy-done.6, bf16[4,8,512,512]{3,2,1,0:T(8,128)(2,1)} %multiply_convert_fusion, bf16[4,512,8,128]{1,0,3,2:T(4,128)(2,1)} %reshape_reshape.3), kind=kOutput, calls=%fused_computation.25 | convolution fusion | flops 2151677952 | bytes 37756928 | tf_op jit(solution)/shard_map/nhts,nthe->nshe/dot_general | solution.py:63
  577.7 11.7 %copy.198 = f32[4,512,8,128]{3,2,1,0:T(8,128)} copy(f32[4,512,8,128]{3,1,2,0:T(8,128)} %add_bitcast_fusion) | data formatting | bytes 16777216 | tf_op jit(solution)/shard_map/add | solution.py:97
  589.4 9.4 %copy.201 = f32[2048,8,128]{0,2,1:T(8,128)} copy(f32[2048,8,128]{2,1,0:T(8,128)} %bitcast.149) | data formatting | bytes 16777216 | tf_op jit(solution)/shard_map/reshape | solution.py:105
  598.9 11.1 %while.63 = (s32[]{:T(128)}, f32[8,128,128]{2,1,0:T(8,128)S(1)}, s32[]{:T(128)}, f32[4,8,128,128]{3,2,1,0:T(8,128)}, f32[4]{0:T(128)S(1)}, /*index=5*/s32[]{:T(128)}, s32[]{:T(128)}, s32[]{:T(128)}, s32[]{:T(128)}, f32[1]{0:T(128)}) while((s32[]{:T(128)}, f32[8,128,128]{2,1,0:T(8,128)S(1)}, s32[]{:T(128)}, ...), condition=%wide.region_9.10_spmd.clone, body=%wide.region_8.9_spmd.clone.sunk | while | flops 524297 | bytes 1573071 | solution.py:26
  610.0 10.9 %fusion.8 = bf16[2048,8,128]{0,2,1:T(8,128)(2,1)} fusion(f32[2048,8,128]{0,2,1:T(8,128)} %copy.190, f32[8,128,128]{2,1,0:T(8,128)S(1)} %get-tuple-element.367, bf16[2048,8,128]{2,1,0:T(8,128)(2,1)} %bitcast.141, f32[2048]{0:T(1024)S(1)} %copy-done.7), kind=kOutput, calls=%fused_computation.20 | convolution fusion | flops 3227516928 | bytes 17309696 | tf_op jit(solution)/shard_map/thf,hef->the/dot_general | solution.py:144
  627.5 11.7 %fusion.7 = bf16[2048,8,128]{0,2,1:T(8,128)(2,1)} fusion(f32[2048,8,128]{0,2,1:T(8,128)} %copy.201, f32[8,128,128]{2,1,0:T(8,128)S(1)} %get-tuple-element.367, bf16[2048,8,128]{2,1,0:T(8,128)(2,1)} %bitcast.143, f32[2048]{0:T(1024)S(1)} %copy-done.7), kind=kOutput, calls=%fused_computation.18 | convolution fusion | flops 3227516928 | bytes 17309696 | tf_op jit(solution)/shard_map/the,hef->thf/dot_general | solution.py:147
  645.6 56.1 %all-reduce.3.cloned.1.call-done = f32[1024,4096]{1,0:T(8,128)} async-done(((f32[1024,4096]{1,0:T(8,128)}), f32[1024,4096]{1,0:T(8,128)}) %all-reduce.3.cloned.1.call-update) | async-done | bytes 16777232 | tf_op jit(solution)/shard_map/psum | solution.py:158
  (116 shorter events, 179.5 us)
Async XLA Ops:
  7.2 124.7 %all-gather.8.cloned.1.call-start = ((), (), s32[]{:S(2)}) async-start(), calls=%async_computation.2 | async-start | bytes 2621440 | tf_op jit(solution)/shard_map/all_gather | solution.py:13
  8.4 5.4 copy-start.5
  16.9 7.6 %copy-start.8 = (s32[1,7]{1,0:T(1,128)S(1)}, s32[1,7]{1,0:T(1,128)}, u32[]{:S(2)}) copy-start(s32[1,7]{1,0:T(1,128)} %param.19) | copy-start | bytes 88
  43.1 0.8 copy-start.1
  43.1 16.7 %copy-start.3 = (f32[4,8,128,128]{3,2,1,0:T(8,128)}, f32[4,8,128,128]{3,2,1,0:T(8,128)S(1)}, u32[]{:S(2)}) copy-start(f32[4,8,128,128]{3,2,1,0:T(8,128)S(1)} %get-tuple-element.362) | copy-start | bytes 6291460
  43.1 3.7 copy-start.11
  43.9 326.4 %all-gather.6.cloned.1.call-start = ((), (), s32[]{:S(2)}) async-start(), calls=%async_computation | async-start | bytes 20971520 | tf_op jit(solution)/shard_map/all_gather | solution.py:121
  44.6 554.2 %all-gather.10.cloned.1.call-start = ((), (), s32[]{:S(2)}) async-start(), calls=%async_computation.3 | async-start | bytes 2621440 | tf_op jit(solution)/shard_map/all_gather | solution.py:13
  86.8 17.2 %copy-start.4 = (f32[4,8,128,128]{3,2,1,0:T(8,128)S(1)}, f32[4,8,128,128]{3,2,1,0:T(8,128)}, u32[]{:S(2)}) copy-start(f32[4,8,128,128]{3,2,1,0:T(8,128)} %copy-done.3) | copy-start | bytes 6291460
  142.8 10.8 %copy-start.9 = (f32[4]{0:T(128)}, f32[4]{0:T(128)S(1)}, u32[]{:S(2)}) copy-start(f32[4]{0:T(128)S(1)} %get-tuple-element.750) | copy-start | bytes 52
  445.9 0.8 copy-start
  446.7 255.0 %all-reduce.3.cloned.1.call-start = ((), (), s32[]{:S(2)}) async-start(), calls=%async_computation.1 | async-start | bytes 33554432 | tf_op jit(solution)/shard_map/psum | solution.py:158
  515.5 11.9 %copy-start.6 = (f32[4,512]{1,0:T(4,128)S(1)}, f32[4,512]{1,0:T(4,128)}, u32[]{:S(2)}) copy-start(f32[4,512]{1,0:T(4,128)} %get-tuple-element.502) | copy-start | bytes 24580
  589.4 9.5 %copy-start.2 = (f32[8,128,128]{2,1,0:T(8,128)S(1)}, f32[8,128,128]{2,1,0:T(8,128)}, u32[]{:S(2)}) copy-start(f32[8,128,128]{2,1,0:T(8,128)} %custom-call.3) | copy-start | bytes 1572868
  589.4 9.5 %copy-start.10 = (f32[4]{0:T(128)S(1)}, f32[4]{0:T(128)}, u32[]{:S(2)}) copy-start(f32[4]{0:T(128)} %copy-done.9) | copy-start | bytes 52
  598.9 11.1 %copy-start.7 = (f32[2048]{0:T(1024)S(1)}, f32[2048]{0:T(1024)}, u32[]{:S(2)}) copy-start(f32[2048]{0:T(1024)} %get-tuple-element.506) | copy-start | bytes 24580
Sparse Core Ops, SparseCore 0:
  44.0 37.8 all-gather.7
  83.5 286.7 all-gather.5
  446.8 33.3 all-gather.9
  483.9 217.7 all-reduce.2
where the time goes:
time: 718 us; the launch traced here: 712 us
  waiting for transfers between devices  273 us (38%)
  matrix products  223 us (31%)
  local copies, waits for them, and re-layouts  147 us (20%)
  other arithmetic  34.7 us (5%)
  between operations  15.6 us (2%)
  blocking collectives  11.7 us (2%)
    all_gather x1, waiting for transfers between devices, on_device(): lax.all_gather(out_cotangent, 'head', axis=2, tiled=True)[0]  217 us
    psum x1, waiting for transfers between devices, on_device(): summed = lax.psum(partial_grad, ('seq', 'rep'))  56.1 us
    unnamed x33, local copies, waits for them, and re-layouts  36.1 us
    dot_general x1, matrix products, on_device(): lax.dot_general(full_cotangent, out_weight, (((1,), (1,)), ((), ())), pre...  24.1 us
    dot_general x1, matrix products, on_device(): lax.dot_general(attention_out, full_cotangent, (((0,), (0,)), ((), ())),...  23.6 us
    dot_general x1, matrix products, local_pass(): jnp.einsum('nhts,nshe->nthe', attn, value_blocks, preferred_element_type=...  17.2 us
    dot_general x1, matrix products, local_pass(): jnp.einsum('nhts,nthe->nshe', attn, grad_blocks, preferred_element_type=j...  17 us
    add x8, other arithmetic, link_step(): return (item[0] + item[1] * state, state)  15 us
  transfers between devices with their start and end apart: 4, of which 2 were waited for; matrix products, arithmetic and copies ran while one was open for 41% of the time, Pallas kernels for 0%

commit v1 on v0

--- a/solution.py
+++ b/solution.py
@@ -155,7 +155,7 @@
     partial_grad = lax.dot_general(
         attention_out, full_cotangent, (((0,), (0,)), ((), ())), preferred_element_type=jnp.float32
     )
-    summed = lax.psum(partial_grad, ("seq", "rep"))
+    summed = jnp.sum(lax.all_gather(partial_grad, ("seq", "rep")), axis=0)
     columns = summed.shape[1] // lax.axis_size(("seq", "rep"))
     grad_weight = lax.dynamic_slice_in_dim(
         summed, lax.axis_index(("seq", "rep")) * columns, columns, 1

time: 718 us -> 1100 us (1.53)
  waiting for transfers between devices: 273 us -> 611 us
  other arithmetic: 34.7 us -> 82 us
    all_gather x0 -> x1, waiting for transfers between devices: none -> 393 us  [on_device(): summed = jnp.sum(lax.all_gather(partial_grad, ('seq', 'rep')), axis=0)]
    psum x1 -> x0, waiting for transfers between devices: 56.1 us -> none  [on_device(): summed = lax.psum(partial_grad, ('seq', 'rep'))]
    reduce_sum x0 -> x1, other arithmetic: none -> 47.2 us  [on_device(): summed = jnp.sum(lax.all_gather(partial_grad, ('seq', 'rep')), axis=0)]
    unnamed x33 -> x31, local copies, waits for them, and re-layouts: 36.1 us -> 36.4 us
  transfers between devices with their start and end apart: 4 -> 4, of which waited for: 2 -> 2; matrix products, arithmetic and copies ran while one was open for 41% -> 29% of each run, Pallas kernels for 0% -> 0%
where the time goes in v1:
time: 1100 us
  waiting for transfers between devices  611 us (56%)
  matrix products  221 us (20%)
  local copies, waits for them, and re-layouts  150 us (14%)
  other arithmetic  82 us (7%)
  between operations  15.6 us (1%)
  blocking collectives  11.6 us (1%)
    all_gather x1, waiting for transfers between devices, on_device(): summed = jnp.sum(lax.all_gather(partial_grad, ('seq', 'rep')), axis=0)  393 us
    all_gather x1, waiting for transfers between devices, on_device(): lax.all_gather(out_cotangent, 'head', axis=2, tiled=True)[0]  217 us
    reduce_sum x1, other arithmetic, on_device(): summed = jnp.sum(lax.all_gather(partial_grad, ('seq', 'rep')), axis=0)  47.2 us
    unnamed x31, local copies, waits for them, and re-layouts  36.4 us
    dot_general x1, matrix products, on_device(): lax.dot_general(full_cotangent, out_weight, (((1,), (1,)), ((), ())), pre...  24.1 us
    dot_general x1, matrix products, on_device(): lax.dot_general(attention_out, full_cotangent, (((0,), (0,)), ((), ())),...  23.7 us
  transfers between devices with their start and end apart: 4, of which 2 were waited for; matrix products, arithmetic and copies ran while one was open for 29% of the time, Pallas kernels for 0%

profile of v1, /device:TPU:0, one launch (start us, length us, event | category | flops | bytes accessed | tf_op | source)
XLA Modules:
  0.0 1096.4 jit_solution(1913916512082089097)
XLA Ops:
  30.3 10.0 while.60
  45.2 11.6 %all-reduce = f32[4]{0:T(128)S(1)} all-reduce(f32[4]{0:T(128)S(1)} %dynamic-update-slice), channel_id=1, replica_groups=mesh['seq'=4,'head'=4,'rep'=2] {'seq'}, use_global_device_ids=true, to_apply=%add | all-reduce | flops 4 | bytes 32
  72.2 11.6 %multiply_convert_fusion = bf16[4,8,512,512]{3,2,1,0:T(8,128)(2,1)} fusion(f32[4,512,512]{2,1,0:T(8,128)} %and_convert_fusion, bf16[4,512,8,128]{1,3,2,0:T(8,128)(2,1)} %copy.184, bf16[4,512,8,128]{1,3,2,0:T(8,128)(2,1)} %copy.175), kind=kOutput, calls=%fused_computation.8 | convolution fusion | flops 2164260864 | bytes 29360128 | tf_op jit(solution)/shard_map/nthe,nshe->nhts/dot_general | solution.py:48
  83.8 17.2 %fusion.24 = f32[4,8,512,128]{3,2,1,0:T(8,128)} fusion(bf16[4,8,512,512]{3,2,1,0:T(8,128)(2,1)} %multiply_convert_fusion, bf16[4,512,8,128]{3,2,1,0:T(8,128)(2,1)} %bitcast.139), kind=kOutput, calls=%fused_computation.39 | convolution fusion | flops 2147483648 | bytes 29360128 | tf_op jit(solution)/shard_map/nhts,nshe->nthe/dot_general | solution.py:56
  128.8 10.9 while.61
  139.7 10.8 fusion.6
  150.5 217.0 %all-gather.8.cloned.1.call-done = bf16[1,2048,4096]{2,1,0:T(8,128)(2,1)} async-done(((bf16[1,2048,1024]{2,1,0:T(8,128)(2,1)}), bf16[1,2048,4096]{2,1,0:T(8,128)(2,1)}) %all-gather.8.cloned.1.call-update) | async-done | bytes 16777232 | tf_op jit(solution)/shard_map/all_gather | solution.py:121
  367.5 24.1 %fusion.17 = bf16[2048,1024]{0,1:T(8,128)(2,1)} fusion(bf16[1024,4096]{1,0:T(8,128)(2,1)} %param.18, bf16[1,2048,4096]{2,1,0:T(8,128)(2,1)} %all-gather.8.cloned.1.call-done), kind=kOutput, calls=%fused_computation.34 | convolution fusion | flops 17181966336 | bytes 29360128 | tf_op jit(solution)/shard_map/dot_general | solution.py:122
  406.3 10.0 while.62
  417.2 23.7 %fusion.2 = f32[1024,4096]{1,0:T(8,128)} fusion(bf16[2048,1024]{0,1:T(8,128)(2,1)} %bitcast.158, bf16[1,2048,4096]{2,1,0:T(8,128)(2,1)} %all-gather.8.cloned.1.call-done), kind=kOutput, calls=%fused_computation.10 | convolution fusion | flops 17179869184 | bytes 37748736 | tf_op jit(solution)/shard_map/dot_general | solution.py:155
  440.9 11.7 %multiply_convert_fusion.1 = bf16[4,8,512,512]{3,2,1,0:T(8,128)(2,1)} fusion(f32[4,512,512]{2,1,0:T(8,128)} %and_convert_fusion, bf16[4,512,8,128]{1,0,3,2:T(4,128)(2,1)} %reshape_reshape.3, bf16[4,512,8,128]{3,2,1,0:T(8,128)(2,1)} %bitcast.140), kind=kOutput, calls=%fused_computation.9 | convolution fusion | flops 2164260864 | bytes 29360128 | tf_op jit(solution)/shard_map/nthe,nshe->nhts/dot_general | solution.py:52
  452.6 13.4 %fusion.35 = f32[4,8,512,128]{3,2,1,0:T(8,128)} fusion(bf16[4,8,512,512]{3,2,1,0:T(8,128)(2,1)} %multiply_convert_fusion.1, bf16[4,512,8,128]{1,3,2,0:T(8,128)(2,1)} %copy.184), kind=kOutput, calls=%fused_computation.63 | convolution fusion | flops 2147483648 | bytes 29360128 | tf_op jit(solution)/shard_map/nhts,nthe->nshe/dot_general | solution.py:60
  466.0 11.9 %bitcast_add_fusion.8 = f32[4,512,8,128]{3,1,2,0:T(8,128)S(1)} fusion(f32[4,8,512,128]{3,2,1,0:T(8,128)} %fusion.35, f32[4,512]{1,0:T(4,128)S(1)} %copy-done.6, f32[4,8,128,128]{3,2,1,0:T(8,128)S(1)} %get-tuple-element.365, bf16[4,512,8,128]{3,2,1,0:T(8,128)(2,1)} %bitcast.141), kind=kOutput, calls=%fused_computation.21 | convolution fusion | flops 3225419776 | bytes 23076864 | tf_op jit(solution)/shard_map/nshf,nhef->nshe/dot_general | solution.py:94
  477.9 10.4 copy.188
  498.2 14.7 %fusion.34 = f32[4,8,512,128]{3,2,1,0:T(8,128)} fusion(bf16[4,8,512,512]{3,2,1,0:T(8,128)(2,1)} %multiply_convert_fusion.1, bf16[4,512,8,128]{1,3,2,0:T(8,128)(2,1)} %copy.175), kind=kOutput, calls=%fused_computation.62 | convolution fusion | flops 2147483648 | bytes 29360128 | tf_op jit(solution)/shard_map/nhts,nshe->nthe/dot_general | solution.py:59
  512.9 10.2 bitcast_add_fusion.10
  540.8 10.5 fusion.9
  565.3 14.8 %add_bitcast_fusion = f32[4,512,8,128]{3,1,2,0:T(8,128)} fusion(f32[4,8,128,512]{2,3,1,0:T(8,128)} %fusion.36, f32[4,512]{1,0:T(4,128)S(1)} %copy-done.6, bf16[4,8,512,512]{3,2,1,0:T(8,128)(2,1)} %multiply_convert_fusion, bf16[4,512,8,128]{1,0,3,2:T(4,128)(2,1)} %reshape_reshape.3), kind=kOutput, calls=%fused_computation.25 | convolution fusion | flops 2151677952 | bytes 37756928 | tf_op jit(solution)/shard_map/nhts,nthe->nshe/dot_general | solution.py:63
  580.1 11.5 %copy.198 = f32[4,512,8,128]{3,2,1,0:T(8,128)} copy(f32[4,512,8,128]{3,1,2,0:T(8,128)} %add_bitcast_fusion) | data formatting | bytes 16777216 | tf_op jit(solution)/shard_map/add | solution.py:97
  601.0 11.0 %while.63 = (s32[]{:T(128)}, f32[8,128,128]{2,1,0:T(8,128)S(1)}, s32[]{:T(128)}, f32[4,8,128,128]{3,2,1,0:T(8,128)}, f32[4]{0:T(128)S(1)}, /*index=5*/s32[]{:T(128)}, s32[]{:T(128)}, s32[]{:T(128)}, s32[]{:T(128)}, f32[1]{0:T(128)}) while((s32[]{:T(128)}, f32[8,128,128]{2,1,0:T(8,128)S(1)}, s32[]{:T(128)}, ...), condition=%wide.region_9.10_spmd.clone, body=%wide.region_8.9_spmd.clone.sunk | while | flops 524297 | bytes 1573071 | solution.py:26
  612.0 10.6 fusion.8
  629.1 10.7 fusion.7
  646.3 393.0 %all-gather.14.cloned.1.call-done = f32[8192,4096]{1,0:T(8,128)} async-done(((f32[1024,4096]{1,0:T(8,128)}), f32[8192,4096]{1,0:T(8,128)}) %all-gather.14.cloned.1.call-update) | async-done | bytes 134217744 | tf_op jit(solution)/shard_map/all_gather | solution.py:158
  1039.2 47.2 %reduce_sum.32 = f32[1024,4096]{1,0:T(8,128)} reduce(f32[8,1024,4096]{2,1,0:T(8,128)} %bitcast.28, f32[]{:T(128)} %constant.146.clone.1), dimensions={0}, to_apply=%region_10.11 | reduce | flops 29360128 | bytes 150994944 | tf_op jit(solution)/shard_map/reduce_sum | solution.py:158
  (115 shorter events, 188.6 us)
Async XLA Ops:
  7.2 121.6 %all-gather.10.cloned.1.call-start = ((), (), s32[]{:S(2)}) async-start(), calls=%async_computation.1 | async-start | bytes 2621440 | tf_op jit(solution)/shard_map/all_gather | solution.py:13
  23.8 3.5 copy-start.1
  27.3 2.8 copy-start
  40.3 0.8 copy-start.3
  40.3 16.5 %copy-start.4 = (f32[4,8,128,128]{3,2,1,0:T(8,128)}, f32[4,8,128,128]{3,2,1,0:T(8,128)S(1)}, u32[]{:S(2)}) copy-start(f32[4,8,128,128]{3,2,1,0:T(8,128)S(1)} %get-tuple-element.362) | copy-start | bytes 6291460
  40.3 3.5 copy-start.10
  41.1 326.4 %all-gather.8.cloned.1.call-start = ((), (), s32[]{:S(2)}) async-start(), calls=%async_computation | async-start | bytes 20971520 | tf_op jit(solution)/shard_map/all_gather | solution.py:121
  41.9 559.1 %all-gather.12.cloned.1.call-start = ((), (), s32[]{:S(2)}) async-start(), calls=%async_computation.2 | async-start | bytes 2621440 | tf_op jit(solution)/shard_map/all_gather | solution.py:13
  83.8 17.2 %copy-start.5 = (f32[4,8,128,128]{3,2,1,0:T(8,128)S(1)}, f32[4,8,128,128]{3,2,1,0:T(8,128)}, u32[]{:S(2)}) copy-start(f32[4,8,128,128]{3,2,1,0:T(8,128)} %copy-done.4) | copy-start | bytes 6291460
  139.7 10.8 copy-start.8
  416.3 0.8 copy-start.2
  417.2 622.1 %all-gather.14.cloned.1.call-start = ((), (), s32[]{:S(2)}) async-start(), calls=%async_computation.3 | async-start | bytes 150994944 | tf_op jit(solution)/shard_map/all_gather | solution.py:158
  452.6 13.4 %copy-start.6 = (f32[4,512]{1,0:T(4,128)S(1)}, f32[4,512]{1,0:T(4,128)}, u32[]{:S(2)}) copy-start(f32[4,512]{1,0:T(4,128)} %get-tuple-element.502) | copy-start | bytes 24580
  591.6 9.4 copy-start.9
  600.9 11.0 %copy-start.7 = (f32[2048]{0:T(1024)S(1)}, f32[2048]{0:T(1024)}, u32[]{:S(2)}) copy-start(f32[2048]{0:T(1024)} %get-tuple-element.506) | copy-start | bytes 24580
Sparse Core Ops, SparseCore 0:
  41.3 37.8 all-gather.9
  80.8 286.7 all-gather.7
  417.3 33.3 all-gather.11
  452.4 586.7 all-gather.13
